TPU v7x, 32 devices: a whole 2x2x4 slice. The times are simulated.
32 devices in a mesh: leaf: 8 (over z, y), row: 4 (over x, core).
Axes of the slice: x: 2, y: 2, z: 4, core: 2. Of those that a mesh axis runs over, the one named last changes fastest.
Arguments:
- panel0: float32 [12288, 512], P(('leaf', 'row')), may hold values from -3 to 30, as said below
- panel1: float32 [6144, 512], P(('leaf', 'row')), may hold values from -3 to 30
- panel2: float32 [3072, 512], P(('leaf', 'row')), may hold values from -3 to 30
- panel3: float32 [1536, 512], P(('leaf', 'row')), may hold values from -3 to 30
- maps1: int32 [8, 8], replicated, may hold values from 0 to 11, as said below
- maps2: int32 [4, 8], replicated, may hold values from 0 to 11, as said below
- maps3: int32 [2, 8], replicated, may hold values from 0 to 11, as said below
Outputs:
- update_top: float32 [1024, 1024], P(('leaf', 'row'))
Inputs may be any that keep to these rules, and one draw needn't show every extreme that they name: `panel0`: each front's first 512 rows form a symmetric matrix, and every assembled pivot block is positive definite. `maps1`: each row lists distinct parent block numbers. `maps2`: each row lists distinct parent block numbers. `maps3`: each row lists distinct parent block numbers.
All inputs are finite; a program needn't handle non-finite values.
Results may differ from a plain program's by a relative error of at most 0.0003.
Values sent between devices are 32-bit elements; how exact they have to be, the bound alone decides.
A program may use at most 128 MiB of HBM per device.

v0:
```python
import jax
import jax.numpy as jnp
from jax import lax
from jax.sharding import PartitionSpec as P

BLOCK = 128
PIV = 512
UPD = 1024
exact_mode = lax.Precision.HIGHEST


def partner(block, axis, stride):
    count = lax.axis_size(axis)
    route = []
    for low in range(count):
        high = low | 1 << stride
        if high != low and high < count:
            route += [(low, high), (high, low)]
    return lax.ppermute(block, axis, route)


def extend_add(update, blocks):
    parent_blocks = (PIV + UPD) // BLOCK
    child_blocks = blocks.shape[0]
    onehot = (blocks[:, None] == jnp.arange(parent_blocks, dtype=jnp.int32)[None, :]).astype(
        jnp.float32
    )
    tile_grid = update.reshape(child_blocks, BLOCK, child_blocks, BLOCK)
    spread = jnp.einsum("ia,ixjy->axjy", onehot, tile_grid, precision=exact_mode)
    placed = jnp.einsum("axjy,jb->axby", spread, onehot, precision=exact_mode)
    return placed.reshape(parent_blocks * BLOCK, parent_blocks * BLOCK)


def exact_dot(left, right):
    return jnp.dot(left, right, precision=exact_mode, preferred_element_type=jnp.float32)


def inverse_factor(pivot_block):
    tile_count = PIV // BLOCK
    identity = jnp.eye(BLOCK, dtype=jnp.float32)
    remaining = pivot_block
    lower_tiles = {}
    diag_inverse = []
    for column_tile in range(tile_count):
        offset = column_tile * BLOCK
        diag_factor = jnp.linalg.cholesky(
            remaining[offset : offset + BLOCK, offset : offset + BLOCK]
        )
        tile_inverse = jax.scipy.linalg.solve_triangular(diag_factor, identity, lower=True)
        diag_inverse.append(tile_inverse)
        if column_tile + 1 < tile_count:
            below_rows = exact_dot(
                remaining[offset + BLOCK :, offset : offset + BLOCK], tile_inverse.T
            )
            for row_tile in range(column_tile + 1, tile_count):
                start_row = (row_tile - column_tile - 1) * BLOCK
                lower_tiles[row_tile, column_tile] = below_rows[start_row : start_row + BLOCK]
            trailing_part = remaining[offset + BLOCK :, offset + BLOCK :] - exact_dot(
                below_rows, below_rows.T
            )
            remaining = remaining.at[offset + BLOCK :, offset + BLOCK :].set(trailing_part)
    inverse_tiles = {}
    for column_tile in range(tile_count):
        inverse_tiles[column_tile, column_tile] = diag_inverse[column_tile]
        for row_tile in range(column_tile + 1, tile_count):
            accumulated = jnp.zeros((BLOCK, BLOCK), jnp.float32)
            for middle in range(column_tile, row_tile):
                accumulated = accumulated + exact_dot(
                    lower_tiles[row_tile, middle], inverse_tiles[middle, column_tile]
                )
            inverse_tiles[row_tile, column_tile] = -exact_dot(diag_inverse[row_tile], accumulated)
    zero_tile = jnp.zeros((BLOCK, BLOCK), jnp.float32)
    tile_rows = []
    for row_tile in range(tile_count):
        pieces = [
            inverse_tiles[row_tile, column_tile] if column_tile <= row_tile else zero_tile
            for column_tile in range(tile_count)
        ]
        tile_rows.append(jnp.concatenate(pieces, axis=1))
    return jnp.concatenate(tile_rows, axis=0)


def group_total(partial_value, level_index):
    portion = lax.psum_scatter(partial_value, "row", scatter_dimension=1, tiled=True)
    for bit_number in range(level_index):
        portion = portion + partner(portion, "leaf", bit_number)
    assembled = lax.all_gather(portion, "row", axis=1, tiled=True)
    return assembled


def body(panel0, panel1, panel2, panel3, maps1, maps2, maps3):
    panels = (panel0, panel1, panel2, panel3)
    block_maps = (maps1, maps1, maps2, maps3)
    row_devices = lax.axis_size("row")
    leaf_index = lax.axis_index("leaf")
    row_index = lax.axis_index("row")
    schur = jnp.zeros((UPD, UPD), jnp.float32)
    for level_index in range(4):
        group_leaves = 2**level_index
        position = leaf_index % group_leaves * row_devices + row_index
        group_devices = group_leaves * row_devices
        panel_rows = panels[level_index]
        row_count = panel_rows.shape[0]
        if level_index == 0:
            partial_value = jnp.zeros((PIV + UPD, PIV), jnp.float32)
            trailing = jnp.zeros((UPD, UPD), jnp.float32)
        else:
            child_front = leaf_index // (group_leaves // 2)
            blocks = lax.dynamic_index_in_dim(
                block_maps[level_index], child_front, 0, keepdims=False
            )
            upper = extend_add(schur, blocks)
            partial_value = upper[:, :PIV]
            trailing = upper[PIV:, PIV:]
        start = position * row_count
        current = lax.dynamic_slice_in_dim(partial_value, start, row_count, 0)
        partial_value = lax.dynamic_update_slice_in_dim(
            partial_value, current + panel_rows, start, 0
        )
        assembled = group_total(partial_value, level_index)
        inverse = inverse_factor(assembled[:PIV])
        column_count = PIV // group_devices
        picked = lax.dynamic_slice_in_dim(inverse, position * column_count, column_count, 0)
        columns = exact_dot(assembled[PIV:], picked.T)
        schur = trailing - exact_dot(columns, columns.T)
    sub_rows = UPD // (8 * row_devices)
    grouped = jnp.swapaxes(schur.reshape(8, row_devices, sub_rows, UPD), 0, 1)
    shared = lax.psum_scatter(grouped, "row", scatter_dimension=0, tiled=True)
    current = shared[0]
    for bit_number in (2, 1, 0):
        half_count = current.shape[0] // 2
        upper_side = leaf_index // 2**bit_number % 2
        lower_half = current[:half_count]
        upper_half = current[half_count:]
        kept_half = jnp.where(upper_side == 1, upper_half, lower_half)
        given_half = jnp.where(upper_side == 1, lower_half, upper_half)
        current = kept_half + partner(given_half, "leaf", bit_number)
    return current.reshape(sub_rows, UPD)


def solution(mesh):
    placed = (
        P(("leaf", "row"), None),
        P(("leaf", "row"), None),
        P(("leaf", "row"), None),
        P(("leaf", "row"), None),
        P(),
        P(),
        P(),
    )
    return jax.shard_map(
        body, mesh=mesh, in_specs=placed, out_specs=P(("leaf", "row"), None), check_vma=False
    )
```

profile of v0, /device:TPU:0, one launch (start us, length us, event | category | flops | bytes accessed | tf_op | source)
XLA Modules:
  0.0 1117.7 jit_solution(9129842647226602034)
XLA Ops:
  12.2 40.7 %reduce-scatter.8.cloned.1.call-done = f32[1536,128]{0,1:T(8,128)} async-done(((f32[1536,512]{0,1:T(8,128)}), f32[1536,128]{0,1:T(8,128)}) %reduce-scatter.8.cloned.1.call-update) | async-done | bytes 786448 | tf_op jit(solution)/shard_map/reduce_scatter | solution.py:84
  54.0 29.0 %all-gather.5.cloned.1.call-done = f32[1536,512]{0,1:T(8,128)} async-done(((f32[1536,128]{0,1:T(8,128)}), f32[1536,512]{0,1:T(8,128)}) %all-gather.5.cloned.1.call-update) | async-done | bytes 3145744 | tf_op jit(solution)/shard_map/all_gather | solution.py:87
  111.2 11.7 %cholesky.265 = f32[128,128]{1,0:T(8,128)S(1)} custom-call(f32[128,128]{1,0:T(8,128)S(1)} %fusion.202), custom_call_target="Cholesky" | custom-call | tf_op jit(solution)/shard_map/jit(cholesky)/cholesky | solution.py:46
  135.7 11.7 %cholesky.276 = f32[128,128]{1,0:T(8,128)S(1)} custom-call(f32[128,128]{1,0:T(8,128)S(1)} %fusion.200), custom_call_target="Cholesky" | custom-call | tf_op jit(solution)/shard_map/jit(cholesky)/cholesky | solution.py:46
  161.2 11.8 %cholesky.287 = f32[128,128]{1,0:T(8,128)S(1)} custom-call(f32[128,128]{1,0:T(8,128)S(1)} %fusion.198), custom_call_target="Cholesky" | custom-call | tf_op jit(solution)/shard_map/jit(cholesky)/cholesky | solution.py:46
  232.9 38.4 %reduce-scatter.10.cloned.1.call-done = f32[1536,128]{0,1:T(8,128)} async-done(((f32[1536,512]{0,1:T(8,128)}), f32[1536,128]{0,1:T(8,128)}) %reduce-scatter.10.cloned.1.call-update) | async-done | bytes 786448 | tf_op jit(solution)/shard_map/reduce_scatter | solution.py:84
  272.8 17.8 %collective-permute-done = f32[1536,128]{0,1:T(8,128)S(1)} collective-permute-done((f32[1536,128]{0,1:T(8,128)}, f32[1536,128]{0,1:T(8,128)S(1)}, u32[]{:S(2)}, u32[]{:S(2)}) %collective-permute-start) | collective-permute-done | bytes 786464 | tf_op jit(solution)/shard_map/ppermute | solution.py:19
  294.6 26.9 %all-gather.7.cloned.1.call-done = f32[1536,512]{0,1:T(8,128)} async-done(((f32[1536,128]{0,1:T(8,128)}), f32[1536,512]{0,1:T(8,128)}) %all-gather.7.cloned.1.call-update) | async-done | bytes 3145744 | tf_op jit(solution)/shard_map/all_gather | solution.py:87
  349.8 11.7 %cholesky.309 = f32[128,128]{1,0:T(8,128)S(1)} custom-call(f32[128,128]{1,0:T(8,128)S(1)} %fusion.194), custom_call_target="Cholesky" | custom-call | tf_op jit(solution)/shard_map/jit(cholesky)/cholesky | solution.py:46
  374.0 11.7 %cholesky.320 = f32[128,128]{1,0:T(8,128)S(1)} custom-call(f32[128,128]{1,0:T(8,128)S(1)} %fusion.192), custom_call_target="Cholesky" | custom-call | tf_op jit(solution)/shard_map/jit(cholesky)/cholesky | solution.py:46
  399.4 12.1 %cholesky.331 = f32[128,128]{1,0:T(8,128)S(1)} custom-call(f32[128,128]{1,0:T(8,128)S(1)} %fusion.190), custom_call_target="Cholesky" | custom-call | tf_op jit(solution)/shard_map/jit(cholesky)/cholesky | solution.py:46
  469.9 38.4 %reduce-scatter.12.cloned.1.call-done = f32[1536,128]{0,1:T(8,128)} async-done(((f32[1536,512]{0,1:T(8,128)}), f32[1536,128]{0,1:T(8,128)}) %reduce-scatter.12.cloned.1.call-update) | async-done | bytes 786448 | tf_op jit(solution)/shard_map/reduce_scatter | solution.py:84
  509.7 17.9 %collective-permute-done.1 = f32[1536,128]{0,1:T(8,128)S(1)} collective-permute-done((f32[1536,128]{0,1:T(8,128)}, f32[1536,128]{0,1:T(8,128)S(1)}, u32[]{:S(2)}, u32[]{:S(2)}) %collective-permute-start.1) | collective-permute-done | bytes 786464 | tf_op jit(solution)/shard_map/ppermute | solution.py:19
  530.4 16.8 %collective-permute-done.2 = f32[1536,128]{0,1:T(8,128)S(1)} collective-permute-done((f32[1536,128]{0,1:T(8,128)S(1)}, f32[1536,128]{0,1:T(8,128)S(1)}, u32[]{:S(2)}, u32[]{:S(2)}) %collective-permute-start.2) | collective-permute-done | bytes 786464 | tf_op jit(solution)/shard_map/ppermute | solution.py:19
  549.6 27.3 %all-gather.9.cloned.1.call-done = f32[1536,512]{0,1:T(8,128)} async-done(((f32[1536,128]{0,1:T(8,128)}), f32[1536,512]{0,1:T(8,128)}) %all-gather.9.cloned.1.call-update) | async-done | bytes 3145744 | tf_op jit(solution)/shard_map/all_gather | solution.py:87
  654.8 11.9 %cholesky.375 = f32[128,128]{1,0:T(8,128)S(1)} custom-call(f32[128,128]{1,0:T(8,128)S(1)} %fusion.182), custom_call_target="Cholesky" | custom-call | tf_op jit(solution)/shard_map/jit(cholesky)/cholesky | solution.py:46
  725.1 38.4 %reduce-scatter.14.cloned.1.call-done = f32[1536,128]{0,1:T(8,128)} async-done(((f32[1536,512]{0,1:T(8,128)}), f32[1536,128]{0,1:T(8,128)}) %reduce-scatter.14.cloned.1.call-update) | async-done | bytes 786448 | tf_op jit(solution)/shard_map/reduce_scatter | solution.py:84
  764.9 17.8 %collective-permute-done.3 = f32[1536,128]{0,1:T(8,128)S(1)} collective-permute-done((f32[1536,128]{0,1:T(8,128)}, f32[1536,128]{0,1:T(8,128)S(1)}, u32[]{:S(2)}, u32[]{:S(2)}) %collective-permute-start.3) | collective-permute-done | bytes 786464 | tf_op jit(solution)/shard_map/ppermute | solution.py:19
  785.6 16.7 %collective-permute-done.4 = f32[1536,128]{0,1:T(8,128)S(1)} collective-permute-done((f32[1536,128]{0,1:T(8,128)S(1)}, f32[1536,128]{0,1:T(8,128)S(1)}, u32[]{:S(2)}, u32[]{:S(2)}) %collective-permute-start.4) | collective-permute-done | bytes 786464 | tf_op jit(solution)/shard_map/ppermute | solution.py:19
  804.9 32.7 %collective-permute-done.5 = f32[1536,128]{0,1:T(8,128)S(1)} collective-permute-done((f32[1536,128]{0,1:T(8,128)S(1)}, f32[1536,128]{0,1:T(8,128)S(1)}, u32[]{:S(2)}, u32[]{:S(2)}) %collective-permute-start.5) | collective-permute-done | bytes 786464 | tf_op jit(solution)/shard_map/ppermute | solution.py:19
  838.9 28.4 %all-gather.11.cloned.1.call-done = f32[1536,512]{0,1:T(8,128)} async-done(((f32[1536,128]{0,1:T(8,128)}), f32[1536,512]{0,1:T(8,128)}) %all-gather.11.cloned.1.call-update) | async-done | bytes 3145744 | tf_op jit(solution)/shard_map/all_gather | solution.py:87
  945.8 11.9 %cholesky.419 = f32[128,128]{1,0:T(8,128)S(1)} custom-call(f32[128,128]{1,0:T(8,128)S(1)} %fusion.174), custom_call_target="Cholesky" | custom-call | tf_op jit(solution)/shard_map/jit(cholesky)/cholesky | solution.py:46
  982.2 84.4 %all-reduce.7.cloned.1.call-done = f32[4,8,32,1024]{3,2,0,1:T(8,128)} async-done(((f32[4,8,32,1024]{3,2,0,1:T(8,128)}), f32[4,8,32,1024]{3,2,0,1:T(8,128)}) %all-reduce.7.cloned.1.call-update) | async-done | bytes 4194320
  1072.9 23.1 %collective-permute-done.6 = f32[4,32,1024]{2,1,0:T(8,128)S(1)} collective-permute-done((f32[4,32,1024]{2,1,0:T(8,128)S(1)}, f32[4,32,1024]{2,1,0:T(8,128)S(1)}, u32[]{:S(2)}, u32[]{:S(2)}) %collective-permute-start.6) | collective-permute-done | bytes 524320 | tf_op jit(solution)/shard_map/ppermute | solution.py:19
  (340 shorter events, 513.2 us)
Async XLA Ops:
  6.5 47.5 %copy-start = (s32[8,8]{1,0:T(8,128)S(1)}, s32[8,8]{1,0:T(8,128)}, u32[]{:S(2)}) copy-start(s32[8,8]{1,0:T(8,128)} %param.38) | copy-start | bytes 772
  6.5 46.4 %reduce-scatter.8.cloned.1.call-start = ((), (), s32[]{:S(2)}) async-start(), calls=%async_computation.4 | async-start | bytes 3932160 | tf_op jit(solution)/shard_map/reduce_scatter | solution.py:84
  8.8 44.2 %copy-start.6 = (f32[192,512]{1,0:T(8,128)S(1)}, f32[192,512]{1,0:T(8,128)}, u32[]{:S(2)}) copy-start(f32[192,512]{1,0:T(8,128)} %param.35) | copy-start | bytes 1179652
  12.1 70.9 %all-gather.5.cloned.1.call-start = ((), (), s32[]{:S(2)}) async-start(), calls=%async_computation.5 | async-start | bytes 3932160 | tf_op jit(solution)/shard_map/all_gather | solution.py:87
  52.9 218.4 %reduce-scatter.10.cloned.1.call-start = ((), (), s32[]{:S(2)}) async-start(), calls=%async_computation.6 | async-start | bytes 3932160 | tf_op jit(solution)/shard_map/reduce_scatter | solution.py:84
  224.4 68.7 %copy-start.7 = (f32[96,512]{1,0:T(8,128)S(1)}, f32[96,512]{1,0:T(8,128)}, u32[]{:S(2)}) copy-start(f32[96,512]{1,0:T(8,128)} %param.36) | copy-start | bytes 589828
  232.9 88.6 %all-gather.7.cloned.1.call-start = ((), (), s32[]{:S(2)}) async-start(), calls=%async_computation.7 | async-start | bytes 3932160 | tf_op jit(solution)/shard_map/all_gather | solution.py:87
  271.3 19.3 %collective-permute-start = (f32[1536,128]{0,1:T(8,128)}, f32[1536,128]{0,1:T(8,128)S(1)}, u32[]{:S(2)}, u32[]{:S(2)}) collective-permute-start(f32[1536,128]{0,1:T(8,128)} %reduce-scatter.10.cloned.1.call-done), channel_id=1, source_target_pairs={{0,4},{4,0},{8,12},{12,8},{16,20},{20,16},{24,28},{28,24},{1,5},{5... | collective-permute-start | bytes 2359304 | tf_op jit(solution)/shard_map/ppermute | solution.py:19
  292.8 215.4 %reduce-scatter.12.cloned.1.call-start = ((), (), s32[]{:S(2)}) async-start(), calls=%async_computation.8 | async-start | bytes 3932160 | tf_op jit(solution)/shard_map/reduce_scatter | solution.py:84
  468.2 80.6 %copy-start.8 = (f32[48,512]{1,0:T(8,128)S(1)}, f32[48,512]{1,0:T(8,128)}, u32[]{:S(2)}) copy-start(f32[48,512]{1,0:T(8,128)} %param.37) | copy-start | bytes 294916
  468.2 81.4 %copy-start.9 = (s32[2,8]{1,0:T(2,128)S(1)}, s32[2,8]{1,0:T(2,128)}, u32[]{:S(2)}) copy-start(s32[2,8]{1,0:T(2,128)} %param.40) | copy-start | bytes 196
  469.8 107.1 %all-gather.9.cloned.1.call-start = ((), (), s32[]{:S(2)}) async-start(), calls=%async_computation.9 | async-start | bytes 3932160 | tf_op jit(solution)/shard_map/all_gather | solution.py:87
  508.3 19.3 %collective-permute-start.1 = (f32[1536,128]{0,1:T(8,128)}, f32[1536,128]{0,1:T(8,128)S(1)}, u32[]{:S(2)}, u32[]{:S(2)}) collective-permute-start(f32[1536,128]{0,1:T(8,128)} %reduce-scatter.12.cloned.1.call-done), channel_id=1, source_target_pairs={{0,4},{4,0},{8,12},{12,8},{16,20},{20,16},{24,28},{28,24},{1,5},{5... | collective-permute-start | bytes 2359304 | tf_op jit(solution)/shard_map/ppermute | solution.py:19
  528.9 18.3 %collective-permute-start.2 = (f32[1536,128]{0,1:T(8,128)S(1)}, f32[1536,128]{0,1:T(8,128)S(1)}, u32[]{:S(2)}, u32[]{:S(2)}) collective-permute-start(f32[1536,128]{0,1:T(8,128)S(1)} %add.230), channel_id=1, source_target_pairs={{0,8},{8,0},{4,12},{12,4},{16,24},{24,16},{20,28},{28,20},{1,9},{9... | collective-permute-start | bytes 2359304 | tf_op jit(solution)/shard_map/ppermute | solution.py:19
  548.2 215.2 %reduce-scatter.14.cloned.1.call-start = ((), (), s32[]{:S(2)}) async-start(), calls=%async_computation.10 | async-start | bytes 3932160 | tf_op jit(solution)/shard_map/reduce_scatter | solution.py:84
  725.0 142.4 %all-gather.11.cloned.1.call-start = ((), (), s32[]{:S(2)}) async-start(), calls=%async_computation.11 | async-start | bytes 3932160 | tf_op jit(solution)/shard_map/all_gather | solution.py:87
  763.4 19.3 %collective-permute-start.3 = (f32[1536,128]{0,1:T(8,128)}, f32[1536,128]{0,1:T(8,128)S(1)}, u32[]{:S(2)}, u32[]{:S(2)}) collective-permute-start(f32[1536,128]{0,1:T(8,128)} %reduce-scatter.14.cloned.1.call-done), channel_id=1, source_target_pairs={{0,4},{4,0},{8,12},{12,8},{16,20},{20,16},{24,28},{28,24},{1,5},{5... | collective-permute-start | bytes 2359304 | tf_op jit(solution)/shard_map/ppermute | solution.py:19
  784.0 18.3 %collective-permute-start.4 = (f32[1536,128]{0,1:T(8,128)S(1)}, f32[1536,128]{0,1:T(8,128)S(1)}, u32[]{:S(2)}, u32[]{:S(2)}) collective-permute-start(f32[1536,128]{0,1:T(8,128)S(1)} %add.241), channel_id=1, source_target_pairs={{0,8},{8,0},{4,12},{12,4},{16,24},{24,16},{20,28},{28,20},{1,9},{9... | collective-permute-start | bytes 2359304 | tf_op jit(solution)/shard_map/ppermute | solution.py:19
  802.4 35.2 %collective-permute-start.5 = (f32[1536,128]{0,1:T(8,128)S(1)}, f32[1536,128]{0,1:T(8,128)S(1)}, u32[]{:S(2)}, u32[]{:S(2)}) collective-permute-start(f32[1536,128]{0,1:T(8,128)S(1)} %add.242), channel_id=1, source_target_pairs={{0,16},{16,0},{4,20},{20,4},{8,24},{24,8},{12,28},{28,12},{1,17},{... | collective-permute-start | bytes 2359304 | tf_op jit(solution)/shard_map/ppermute | solution.py:19
  838.7 228.0 %all-reduce.7.cloned.1.call-start = ((), (), s32[]{:S(2)}) async-start(), calls=%async_computation.12 | async-start | bytes 8388608
  1066.6 44.3 %copy-start.1 = (s32[8,8]{1,0:T(8,128)S(1)}, s32[8,8]{1,0:T(8,128)}, u32[]{:S(2)}) copy-start(s32[8,8]{1,0:T(8,128)} %param.38) | copy-start | bytes 772
  1070.4 25.5 %collective-permute-start.6 = (f32[4,32,1024]{2,1,0:T(8,128)S(1)}, f32[4,32,1024]{2,1,0:T(8,128)S(1)}, u32[]{:S(2)}, u32[]{:S(2)}) collective-permute-start(f32[4,32,1024]{2,1,0:T(8,128)S(1)} %fusion.22), channel_id=1, source_target_pairs={{0,16},{16,0},{4,20},{20,4},{8,24},{24,8},{12,28},{28,12},{1,17},{... | collective-permute-start | bytes 1572872 | tf_op jit(solution)/shard_map/ppermute | solution.py:19
  1097.8 7.4 collective-permute-start.7
  1105.3 5.0 collective-permute-start.8
  (5 other events, 7.2 us)
Sparse Core Ops, SparseCore 0:
  12.3 40.5 reduce-scatter.7
  54.5 28.5 all-gather.4
  233.0 38.2 reduce-scatter.9
  293.0 28.5 all-gather.6
  469.9 38.2 reduce-scatter.11
  548.4 28.4 all-gather.8
  725.1 38.2 reduce-scatter.13
  838.8 28.5 all-gather.10
  981.1 85.4 all-reduce.6
where the time goes:
time: 1130 us; the launch traced here: 1120 us
  waiting for transfers between devices  505 us (45%)
  other arithmetic  388 us (34%)
  matrix products  115 us (10%)
  local copies, waits for them, and re-layouts  78.7 us (7%)
  starting transfers between devices  15.7 us (1%)
  between operations  15.2 us (1%)
    another operation x48, other arithmetic, inverse_factor(): jnp.linalg.cholesky(remaining[offset:offset + BLOCK, offset:offset + BLOCK])  199 us
    another operation x32, other arithmetic, inverse_factor(): jax.scipy.linalg.solve_triangular(diag_factor, identity, lower=True)  169 us
    reduce_scatter x4, waiting for transfers between devices, group_total(): lax.psum_scatter(partial_value, 'row', scatter_dimension=1, tiled=True)  156 us
    ppermute x9, waiting for transfers between devices, partner(): return lax.ppermute(block, axis, route)  153 us
    all_gather x4, waiting for transfers between devices, group_total(): assembled = lax.all_gather(portion, 'row', axis=1, tiled=True)  112 us
    unnamed x10, waiting for transfers between devices  84.6 us
    dot_general x96, matrix products, exact_dot(): jnp.dot(left, right, precision=exact_mode, preferred_element_type=jnp.flo...  72.2 us
    unnamed x36, local copies, waits for them, and re-layouts  47.8 us
  transfers between devices with their start and end apart: 18, of which 18 were waited for; matrix products, arithmetic and copies ran while one was open for 0% of the time, Pallas kernels for 0%

commit v1 on v0

--- a/solution.py
+++ b/solution.py
@@ -84,7 +84,14 @@
     portion = lax.psum_scatter(partial_value, "row", scatter_dimension=1, tiled=True)
     for bit_number in range(level_index):
         portion = portion + partner(portion, "leaf", bit_number)
-    assembled = lax.all_gather(portion, "row", axis=1, tiled=True)
+    ways = lax.axis_size("row")
+    pieces_2 = [portion]
+    for far in range(1, ways):
+        pieces_2.append(
+            lax.ppermute(pieces_2[far - 1], "row", [(d, (d - 1) % ways) for d in range(ways)])
+        )
+    line = jnp.concatenate(pieces_2, axis=1)
+    assembled = jnp.roll(line, lax.axis_index("row") * portion.shape[1], axis=1)
     return assembled
 
 

time: 1130 us -> 1320 us (1.17)
  matrix products: 115 us -> 182 us
  other arithmetic: 388 us -> 450 us
  local copies, waits for them, and re-layouts: 78.7 us -> 117 us
  starting transfers between devices: 15.7 us -> 29.9 us
    all_gather x4 -> x0, waiting for transfers between devices: 112 us -> none  [group_total(): assembled = lax.all_gather(portion, 'row', axis=1, tiled=True)]
    ppermute x0 -> x12, waiting for transfers between devices: none -> 111 us  [group_total(): lax.ppermute(pieces_2[far - 1], 'row', [(d, (d - 1) % ways) for d in rang...]
    dot_general x96, matrix products: 72.2 us -> 132 us  [exact_dot(): jnp.dot(left, right, precision=exact_mode, preferred_element_type=jnp.flo...]
    another operation x32, other arithmetic: 169 us -> 189 us  [inverse_factor(): jax.scipy.linalg.solve_triangular(diag_factor, identity, lower=True)]
    concatenate x0 -> x4, other arithmetic: none -> 18 us  [group_total(): assembled = jnp.roll(line, lax.axis_index('row') * portion.shape[1], axis=1)]
    another operation x48, other arithmetic: 199 us -> 216 us  [inverse_factor(): jnp.linalg.cholesky(remaining[offset:offset + BLOCK, offset:offset + BLOCK])]
    ppermute x0 -> x12, starting transfers between devices: none -> 15.2 us  [group_total(): lax.ppermute(pieces_2[far - 1], 'row', [(d, (d - 1) % ways) for d in rang...]
    unnamed x36 -> x106, local copies, waits for them, and re-layouts: 47.8 us -> 63 us
  transfers between devices with their start and end apart: 18 -> 26, of which waited for: 18 -> 26; matrix products, arithmetic and copies ran while one was open for 0% -> 0% of each run, Pallas kernels for 0% -> 0%
where the time goes in v1:
time: 1320 us; the launch traced here: 1310 us
  waiting for transfers between devices  513 us (39%)
  other arithmetic  450 us (34%)
  matrix products  182 us (14%)
  local copies, waits for them, and re-layouts  117 us (9%)
  starting transfers between devices  29.9 us (2%)
  between operations  14.9 us (1%)
    another operation x48, other arithmetic, inverse_factor(): jnp.linalg.cholesky(remaining[offset:offset + BLOCK, offset:offset + BLOCK])  216 us
    another operation x32, other arithmetic, inverse_factor(): jax.scipy.linalg.solve_triangular(diag_factor, identity, lower=True)  189 us
    reduce_scatter x4, waiting for transfers between devices, group_total(): lax.psum_scatter(partial_value, 'row', scatter_dimension=1, tiled=True)  162 us
    ppermute x9, waiting for transfers between devices, partner(): return lax.ppermute(block, axis, route)  153 us
    dot_general x96, matrix products, exact_dot(): jnp.dot(left, right, precision=exact_mode, preferred_element_type=jnp.flo...  132 us
    ppermute x12, waiting for transfers between devices, group_total(): lax.ppermute(pieces_2[far - 1], 'row', [(d, (d - 1) % ways) for d in rang...  111 us
    unnamed x6, waiting for transfers between devices  86.9 us
    unnamed x106, local copies, waits for them, and re-layouts  63 us
  transfers between devices with their start and end apart: 26, of which 26 were waited for; matrix products, arithmetic and copies ran while one was open for 0% of the time, Pallas kernels for 0%

profile of v1, /device:TPU:0, one launch (start us, length us, event | category | flops | bytes accessed | tf_op | source)
XLA Modules:
  0.0 1306.5 jit_solution(7443900182954735374)
XLA Ops:
  11.8 40.7 %reduce-scatter.8.cloned.1.call-done = f32[1536,128]{0,1:T(8,128)} async-done(((f32[1536,512]{0,1:T(8,128)}), f32[1536,128]{0,1:T(8,128)}) %reduce-scatter.8.cloned.1.call-update) | async-done | bytes 786448 | tf_op jit(solution)/shard_map/reduce_scatter | solution.py:84
  90.6 11.7 cholesky.254
  148.0 13.2 %cholesky.276 = f32[128,128]{1,0:T(8,128)} custom-call(f32[128,128]{1,0:T(8,128)} %fusion.228), custom_call_target="Cholesky" | custom-call | tf_op jit(solution)/shard_map/jit(cholesky)/cholesky | solution.py:46
  191.9 11.9 cholesky.287
  269.6 40.7 %reduce-scatter.10.cloned.1.call-done = f32[1536,128]{0,1:T(8,128)} async-done(((f32[1536,512]{0,1:T(8,128)}), f32[1536,128]{0,1:T(8,128)}) %reduce-scatter.10.cloned.1.call-update) | async-done | bytes 786448 | tf_op jit(solution)/shard_map/reduce_scatter | solution.py:84
  311.8 17.9 %collective-permute-done.3 = f32[1536,128]{0,1:T(8,128)S(1)} collective-permute-done((f32[1536,128]{0,1:T(8,128)}, f32[1536,128]{0,1:T(8,128)S(1)}, u32[]{:S(2)}, u32[]{:S(2)}) %collective-permute-start.3) | collective-permute-done | bytes 786464 | tf_op jit(solution)/shard_map/ppermute | solution.py:19
  369.6 11.7 cholesky.298
  426.8 13.2 %cholesky.320 = f32[128,128]{1,0:T(8,128)} custom-call(f32[128,128]{1,0:T(8,128)} %fusion.220), custom_call_target="Cholesky" | custom-call | tf_op jit(solution)/shard_map/jit(cholesky)/cholesky | solution.py:46
  472.0 13.5 %cholesky.331 = f32[128,128]{1,0:T(8,128)} custom-call(f32[128,128]{1,0:T(8,128)} %fusion.218), custom_call_target="Cholesky" | custom-call | tf_op jit(solution)/shard_map/jit(cholesky)/cholesky | solution.py:46
  556.4 40.2 %reduce-scatter.12.cloned.1.call-done = f32[1536,128]{0,1:T(8,128)} async-done(((f32[1536,512]{0,1:T(8,128)}), f32[1536,128]{0,1:T(8,128)}) %reduce-scatter.12.cloned.1.call-update) | async-done | bytes 786448 | tf_op jit(solution)/shard_map/reduce_scatter | solution.py:84
  598.1 17.8 %collective-permute-done.7 = f32[1536,128]{0,1:T(8,128)S(1)} collective-permute-done((f32[1536,128]{0,1:T(8,128)}, f32[1536,128]{0,1:T(8,128)S(1)}, u32[]{:S(2)}, u32[]{:S(2)}) %collective-permute-start.7) | collective-permute-done | bytes 786464 | tf_op jit(solution)/shard_map/ppermute | solution.py:19
  618.7 16.8 %collective-permute-done.8 = f32[1536,128]{0,1:T(8,128)S(1)} collective-permute-done((f32[1536,128]{0,1:T(8,128)S(1)}, f32[1536,128]{0,1:T(8,128)S(1)}, u32[]{:S(2)}, u32[]{:S(2)}) %collective-permute-start.8) | collective-permute-done | bytes 786464 | tf_op jit(solution)/shard_map/ppermute | solution.py:19
  674.5 11.7 cholesky.342
  731.7 13.2 %cholesky.364 = f32[128,128]{1,0:T(8,128)} custom-call(f32[128,128]{1,0:T(8,128)} %fusion.212), custom_call_target="Cholesky" | custom-call | tf_op jit(solution)/shard_map/jit(cholesky)/cholesky | solution.py:46
  776.9 13.4 %cholesky.375 = f32[128,128]{1,0:T(8,128)} custom-call(f32[128,128]{1,0:T(8,128)} %fusion.210), custom_call_target="Cholesky" | custom-call | tf_op jit(solution)/shard_map/jit(cholesky)/cholesky | solution.py:46
  861.1 40.1 %reduce-scatter.14.cloned.1.call-done = f32[1536,128]{0,1:T(8,128)} async-done(((f32[1536,512]{0,1:T(8,128)}), f32[1536,128]{0,1:T(8,128)}) %reduce-scatter.14.cloned.1.call-update) | async-done | bytes 786448 | tf_op jit(solution)/shard_map/reduce_scatter | solution.py:84
  902.8 17.8 %collective-permute-done.12 = f32[1536,128]{0,1:T(8,128)S(1)} collective-permute-done((f32[1536,128]{0,1:T(8,128)}, f32[1536,128]{0,1:T(8,128)S(1)}, u32[]{:S(2)}, u32[]{:S(2)}) %collective-permute-start.12) | collective-permute-done | bytes 786464 | tf_op jit(solution)/shard_map/ppermute | solution.py:19
  923.4 16.8 %collective-permute-done.13 = f32[1536,128]{0,1:T(8,128)S(1)} collective-permute-done((f32[1536,128]{0,1:T(8,128)S(1)}, f32[1536,128]{0,1:T(8,128)S(1)}, u32[]{:S(2)}, u32[]{:S(2)}) %collective-permute-start.13) | collective-permute-done | bytes 786464 | tf_op jit(solution)/shard_map/ppermute | solution.py:19
  942.7 32.7 %collective-permute-done.14 = f32[1536,128]{0,1:T(8,128)S(1)} collective-permute-done((f32[1536,128]{0,1:T(8,128)S(1)}, f32[1536,128]{0,1:T(8,128)S(1)}, u32[]{:S(2)}, u32[]{:S(2)}) %collective-permute-start.14) | collective-permute-done | bytes 786464 | tf_op jit(solution)/shard_map/ppermute | solution.py:19
  1014.3 11.7 cholesky.386
  1077.8 13.2 %cholesky.408 = f32[128,128]{1,0:T(8,128)} custom-call(f32[128,128]{1,0:T(8,128)} %fusion.204), custom_call_target="Cholesky" | custom-call | tf_op jit(solution)/shard_map/jit(cholesky)/cholesky | solution.py:46
  1117.9 13.3 %cholesky.419 = f32[128,128]{1,0:T(8,128)} custom-call(f32[128,128]{1,0:T(8,128)} %fusion.202), custom_call_target="Cholesky" | custom-call | tf_op jit(solution)/shard_map/jit(cholesky)/cholesky | solution.py:46
  1168.6 86.8 %all-reduce.7.cloned.1.call-done = f32[4,8,32,1024]{3,2,0,1:T(8,128)} async-done(((f32[4,8,32,1024]{3,2,0,1:T(8,128)}), f32[4,8,32,1024]{3,2,0,1:T(8,128)}) %all-reduce.7.cloned.1.call-update) | async-done | bytes 4194320
  1261.7 23.1 %collective-permute-done.18 = f32[4,32,1024]{2,1,0:T(8,128)S(1)} collective-permute-done((f32[4,32,1024]{2,1,0:T(8,128)S(1)}, f32[4,32,1024]{2,1,0:T(8,128)S(1)}, u32[]{:S(2)}, u32[]{:S(2)}) %collective-permute-start.18) | collective-permute-done | bytes 524320 | tf_op jit(solution)/shard_map/ppermute | solution.py:19
  (426 shorter events, 748.6 us)
Async XLA Ops:
  6.5 46.0 %reduce-scatter.8.cloned.1.call-start = ((), (), s32[]{:S(2)}) async-start(), calls=%async_computation.4 | async-start | bytes 3932160 | tf_op jit(solution)/shard_map/reduce_scatter | solution.py:84
  11.8 298.5 %reduce-scatter.10.cloned.1.call-start = ((), (), s32[]{:S(2)}) async-start(), calls=%async_computation.5 | async-start | bytes 3932160 | tf_op jit(solution)/shard_map/reduce_scatter | solution.py:84
  52.5 9.8 collective-permute-start
  63.2 11.3 collective-permute-start.1
  74.5 11.4 collective-permute-start.2
  269.6 327.0 %reduce-scatter.12.cloned.1.call-start = ((), (), s32[]{:S(2)}) async-start(), calls=%async_computation.6 | async-start | bytes 3932160 | tf_op jit(solution)/shard_map/reduce_scatter | solution.py:84
  310.3 19.4 %collective-permute-start.3 = (f32[1536,128]{0,1:T(8,128)}, f32[1536,128]{0,1:T(8,128)S(1)}, u32[]{:S(2)}, u32[]{:S(2)}) collective-permute-start(f32[1536,128]{0,1:T(8,128)} %reduce-scatter.10.cloned.1.call-done), channel_id=1, source_target_pairs={{0,4},{4,0},{8,12},{12,8},{16,20},{20,16},{24,28},{28,24},{1,5},{5... | collective-permute-start | bytes 2359304 | tf_op jit(solution)/shard_map/ppermute | solution.py:19
  331.8 9.5 collective-permute-start.4
  342.2 11.4 collective-permute-start.5
  353.6 11.4 collective-permute-start.6
  556.4 344.9 %reduce-scatter.14.cloned.1.call-start = ((), (), s32[]{:S(2)}) async-start(), calls=%async_computation.7 | async-start | bytes 3932160 | tf_op jit(solution)/shard_map/reduce_scatter | solution.py:84
  596.6 19.3 %collective-permute-start.7 = (f32[1536,128]{0,1:T(8,128)}, f32[1536,128]{0,1:T(8,128)S(1)}, u32[]{:S(2)}, u32[]{:S(2)}) collective-permute-start(f32[1536,128]{0,1:T(8,128)} %reduce-scatter.12.cloned.1.call-done), channel_id=1, source_target_pairs={{0,4},{4,0},{8,12},{12,8},{16,20},{20,16},{24,28},{28,24},{1,5},{5... | collective-permute-start | bytes 2359304 | tf_op jit(solution)/shard_map/ppermute | solution.py:19
  617.2 18.3 %collective-permute-start.8 = (f32[1536,128]{0,1:T(8,128)S(1)}, f32[1536,128]{0,1:T(8,128)S(1)}, u32[]{:S(2)}, u32[]{:S(2)}) collective-permute-start(f32[1536,128]{0,1:T(8,128)S(1)} %add.238), channel_id=1, source_target_pairs={{0,8},{8,0},{4,12},{12,4},{16,24},{24,16},{20,28},{28,20},{1,9},{9... | collective-permute-start | bytes 2359304 | tf_op jit(solution)/shard_map/ppermute | solution.py:19
  636.5 9.5 collective-permute-start.9
  646.9 11.4 collective-permute-start.10
  658.3 11.4 collective-permute-start.11
  861.1 394.3 %all-reduce.7.cloned.1.call-start = ((), (), s32[]{:S(2)}) async-start(), calls=%async_computation.8 | async-start | bytes 8388608
  901.3 19.3 %collective-permute-start.12 = (f32[1536,128]{0,1:T(8,128)}, f32[1536,128]{0,1:T(8,128)S(1)}, u32[]{:S(2)}, u32[]{:S(2)}) collective-permute-start(f32[1536,128]{0,1:T(8,128)} %reduce-scatter.14.cloned.1.call-done), channel_id=1, source_target_pairs={{0,4},{4,0},{8,12},{12,8},{16,20},{20,16},{24,28},{28,24},{1,5},{5... | collective-permute-start | bytes 2359304 | tf_op jit(solution)/shard_map/ppermute | solution.py:19
  921.9 18.3 %collective-permute-start.13 = (f32[1536,128]{0,1:T(8,128)S(1)}, f32[1536,128]{0,1:T(8,128)S(1)}, u32[]{:S(2)}, u32[]{:S(2)}) collective-permute-start(f32[1536,128]{0,1:T(8,128)S(1)} %add.249), channel_id=1, source_target_pairs={{0,8},{8,0},{4,12},{12,4},{16,24},{24,16},{20,28},{28,20},{1,9},{9... | collective-permute-start | bytes 2359304 | tf_op jit(solution)/shard_map/ppermute | solution.py:19
  940.3 35.2 %collective-permute-start.14 = (f32[1536,128]{0,1:T(8,128)S(1)}, f32[1536,128]{0,1:T(8,128)S(1)}, u32[]{:S(2)}, u32[]{:S(2)}) collective-permute-start(f32[1536,128]{0,1:T(8,128)S(1)} %add.250), channel_id=1, source_target_pairs={{0,16},{16,0},{4,20},{20,4},{8,24},{24,8},{12,28},{28,12},{1,17},{... | collective-permute-start | bytes 2359304 | tf_op jit(solution)/shard_map/ppermute | solution.py:19
  976.5 9.5 collective-permute-start.15
  986.9 11.4 collective-permute-start.16
  998.3 11.4 collective-permute-start.17
  1259.2 25.5 %collective-permute-start.18 = (f32[4,32,1024]{2,1,0:T(8,128)S(1)}, f32[4,32,1024]{2,1,0:T(8,128)S(1)}, u32[]{:S(2)}, u32[]{:S(2)}) collective-permute-start(f32[4,32,1024]{2,1,0:T(8,128)S(1)} %fusion.50), channel_id=1, source_target_pairs={{0,16},{16,0},{4,20},{20,4},{8,24},{24,8},{12,28},{28,12},{1,17},{... | collective-permute-start | bytes 1572872 | tf_op jit(solution)/shard_map/ppermute | solution.py:19
  (48 other events, 557.8 us)
Sparse Core Ops, SparseCore 0:
  11.9 40.5 reduce-scatter.7
  269.7 40.5 reduce-scatter.9
  556.5 40.0 reduce-scatter.11
  861.2 40.0 reduce-scatter.13
  1167.5 87.8 all-reduce.6
